TPU v7x, 256 devices: a whole 4x4x8 slice. The times are simulated.
256 devices in a mesh: fsdp: 64 (over x_hi, z, y), grp: 4 (over x_lo, core).
Axes of the slice: x: 4 (x_hi: 2, x_lo: 2; x = x_hi * 2 + x_lo), y: 4, z: 8, core: 2. Of those that a mesh axis runs over, the one named last changes fastest.
Arguments:
- weight: bfloat16 [26624, 8192], P('fsdp', 'grp'), may hold values from -6 to 6
Outputs:
- quantized: bfloat16 [26624, 8192], P('grp', 'fsdp')
- scales: float32 [208, 64], P('grp', 'fsdp')
All inputs are finite; a program needn't handle non-finite values. Where the computation divides by a largest or mean magnitude, that divisor is 1e-20 or more.
Results may differ from a plain program's by a relative error of at most 0.001.
Values sent between devices are 32-bit elements; how exact they have to be, the bound alone decides.
A program may use at most 128 MiB of HBM per device.

v0:
```python
import math

import jax
import jax.numpy as jnp
import numpy as np
from jax import lax
from jax.sharding import PartitionSpec as P

D = 8192
BLOCK = 128
FF = 26624


def paley_signs():
    squares_set = set()
    for coord_one in range(5):
        for coord_two in range(5):
            if coord_one or coord_two:
                squares_set.add(
                    (
                        (coord_one * coord_one + 2 * coord_two * coord_two) % 5,
                        2 * coord_one * coord_two % 5,
                    )
                )
    conference = np.zeros((26, 26), np.float32)
    conference[0, 1:] = 1.0
    conference[1:, 0] = 1.0
    for row_elem in range(25):
        for col_elem in range(25):
            diff_one = (row_elem % 5 - col_elem % 5) % 5
            diff_two = (row_elem // 5 - col_elem // 5) % 5
            if diff_one or diff_two:
                conference[1 + row_elem, 1 + col_elem] = (
                    1.0 if (diff_one, diff_two) in squares_set else -1.0
                )
    plus_block = np.array([[1.0, 1.0], [1.0, -1.0]], np.float32)
    minus_block = np.array([[1.0, -1.0], [-1.0, -1.0]], np.float32)
    return (
        np.kron(conference, plus_block) + np.kron(np.eye(26, dtype=np.float32), minus_block)
    ).astype(np.float32)


def sign_table(order, dtype):
    indices = lax.iota(jnp.int32, order)
    parity = jnp.zeros((order, order), jnp.int32)
    for bit_pos in range(max(order.bit_length() - 1, 0)):
        parity = parity + (indices[:, None] >> bit_pos & 1) * (indices[None, :] >> bit_pos & 1)
    return (1 - 2 * (parity & 1)).astype(dtype)


def body(weight):
    exact_prec = lax.Precision.HIGHEST
    rows_dev, cols_dev = weight.shape
    parts = lax.axis_size("fsdp")
    groups = lax.axis_size("grp")
    sub_rows = rows_dev // 52
    piece = cols_dev // parts
    piece_signs = sign_table(piece, jnp.bfloat16)
    parts_signs = sign_table(parts, jnp.float32)
    paley = jnp.asarray(paley_signs(), jnp.float32)
    sub_signs = sign_table(sub_rows, jnp.float32)
    group_signs = sign_table(groups, jnp.float32)
    inner_done = jnp.einsum(
        "rab,bj->raj",
        weight.reshape(rows_dev, parts, piece),
        piece_signs,
        preferred_element_type=jnp.float32,
    )
    rotated = jnp.einsum("ap,raj->prj", parts_signs, inner_done, precision=exact_prec)
    rotated = rotated.reshape(parts, sub_rows, 52, piece)
    rotated = jnp.einsum("ab,pcbj->pcaj", paley, rotated, precision=exact_prec)
    rotated = jnp.einsum("ce,peaj->pcaj", sub_signs, rotated, precision=exact_prec)
    rotated = rotated.reshape(parts, sub_rows, 52 * piece)
    fsdp_signs = sign_table(parts, jnp.float32)
    mixed = jnp.einsum(
        "fg,gnx->fnx",
        fsdp_signs,
        lax.all_to_all(rotated, "fsdp", split_axis=0, concat_axis=0, tiled=True),
        precision=exact_prec,
    )
    count = mixed.shape[1]
    stacked = mixed.reshape(1, parts, count, 52 * piece)
    moved = lax.all_to_all(stacked, "grp", split_axis=1, concat_axis=0, tiled=True)
    moved = moved.reshape(groups, parts // groups, count, 52, piece)
    result = jnp.einsum("qg,gmnaj->mnaqj", group_signs, moved, precision=exact_prec)
    cols_out = groups * piece
    final = result.reshape(-1, cols_out) * (1.0 / math.sqrt(FF * D))
    rows_out = final.shape[0]
    blocks = final.reshape(rows_out // BLOCK, BLOCK, cols_out // BLOCK, BLOCK)
    scales = jnp.max(jnp.abs(blocks), axis=(1, 3))
    quantized = (
        (blocks / (scales[:, None, :, None] + 1e-06))
        .astype(jnp.bfloat16)
        .reshape(rows_out, cols_out)
    )
    return (quantized, scales)


def solution(mesh):
    in_specs = (P("fsdp", "grp"),)
    out_specs = (P("grp", "fsdp"), P("grp", "fsdp"))
    return jax.shard_map(body, mesh=mesh, in_specs=in_specs, out_specs=out_specs, check_vma=False)
```

profile of v0, /device:TPU:1, one launch (start us, length us, event | category | flops | bytes accessed | tf_op | source)
XLA Modules:
  0.0 280.0 jit_solution(4286897665663929266)
XLA Ops:
  0.7 2.8 copy.27
  3.5 0.8 convolution_bitcast_fusion
  4.3 7.2 %fusion.4 = f32[64,416,32]{1,0,2:T(8,128)} fusion(f32[416,64,32]{0,2,1:T(8,128)S(1)} %convolution_bitcast_fusion, s32[64]{0:T(128)S(1)} %get-tuple-element.14, s32[64]{0:T(128)S(1)} %get-tuple-element.15, s32[64]{0:T(128)S(1)} %get-tuple-element.16, s32[64]{0:T(128)S(1)} %get-tuple-element.17, s32[64]{0:T(128)S(1)} %get-tuple-element.18, ...), kind=kOutput, calls=%fused_computation.6 | convolution fusion | flops 654372864 | bytes 6817280 | tf_op jit(solution)/shard_map/ap,raj->prj/dot_general | solution.py:69
  11.4 0.0 copy-start
  11.4 8.0 %reshape.284 = f32[64,8,52,32]{2,1,0,3:T(8,128)} reshape(f32[64,416,32]{1,0,2:T(8,128)} %fusion.4) | data formatting | bytes 6815744 | tf_op jit(solution)/shard_map/reshape | solution.py:70
  19.4 0.0 copy-done
  19.5 27.0 %fusion.11 = f32[64,8,52,32]{0,2,3,1:T(8,128)S(1)} fusion(f32[52,52,1,1]{1,0,3,2:T(8,128)S(1)} %copy-done, f32[64,8,52,32]{2,1,0,3:T(8,128)} %reshape.284), kind=kOutput, calls=%fused_computation.12 | convolution fusion | flops 531628032 | bytes 6826560 | tf_op jit(solution)/shard_map/ab,pcbj->pcaj/dot_general | solution.py:71
  46.5 10.6 %fusion.2 = f32[64,52,32,8]{0,3,2,1:T(8,128)} fusion(f32[64,8,52,32]{0,2,3,1:T(8,128)S(1)} %fusion.11, s32[8]{0:T(128)S(1)} %get-tuple-element.20, s32[8]{0:T(128)S(1)} %get-tuple-element.21, s32[8]{0:T(128)S(1)} %shift-right-arithmetic_and_fusion.4), kind=kOutput, calls=%fused_computation.4 | convolution fusion | flops 81789504 | bytes 6815840 | tf_op jit(solution)/shard_map/ce,peaj->pcaj/dot_general | solution.py:72
  57.1 6.4 %copy.33 = f32[64,8,1664]{2,1,0:T(8,128)S(1)} copy(f32[64,8,1664]{0,1,2:T(8,128)} %bitcast.52) | data formatting | bytes 6815744 | tf_op jit(solution)/shard_map/reshape | solution.py:73
  63.5 93.5 %all_to_all.14 = f32[64,8,1664]{2,1,0:T(8,128)S(1)} all-to-all(f32[64,8,1664]{2,1,0:T(8,128)S(1)} %copy.33), channel_id=1, replica_groups=mesh['fsdp'=64,'grp'=4] {'fsdp'}, dimensions={0} | all-to-all | bytes 6815744 | tf_op jit(solution)/shard_map/all_to_all | solution.py:78
  157.0 3.6 %fusion.8 = f32[1,64,8,1664]{3,1,2,0:T(8,128)S(1)} fusion(f32[64,8,1664]{2,1,0:T(8,128)S(1)} %all_to_all.14, s32[64]{0:T(128)S(1)} %get-tuple-element.14, s32[64]{0:T(128)S(1)} %get-tuple-element.15, s32[64]{0:T(128)S(1)} %get-tuple-element.16, s32[64]{0:T(128)S(1)} %get-tuple-element.17, s32[64]{0:T(128)S(1)} %get-tuple-element.18, ...), kind=kOutput, calls=%fused_computation.11 | convolution fusion | flops 654372864 | bytes 6817280 | tf_op jit(solution)/shard_map/fg,gnx->fnx/dot_general | solution.py:75
  160.6 3.7 %copy.35 = f32[1,64,8,1664]{3,2,0,1:T(8,128)} copy(f32[1,64,8,1664]{3,1,2,0:T(8,128)S(1)} %fusion.8) | data formatting | bytes 6815744 | tf_op jit(solution)/shard_map/reshape | solution.py:82
  164.3 6.8 %all-to-all-start.1 = ((f32[1,64,8,1664]{3,2,0,1:T(8,128)}), f32[1,64,8,1664]{3,2,0,1:T(8,128)S(1)}, u32[]{:S(2)}, u32[]{:S(2)}) async-start(f32[1,64,8,1664]{3,2,0,1:T(8,128)} %copy.35), calls=%async_computation.1 | async-start | bytes 6815744 | tf_op jit(solution)/shard_map/all_to_all | solution.py:83
  171.1 38.7 %all-to-all-done.1 = f32[1,64,8,1664]{3,2,0,1:T(8,128)S(1)} async-done(((f32[1,64,8,1664]{3,2,0,1:T(8,128)}), f32[1,64,8,1664]{3,2,0,1:T(8,128)S(1)}, u32[]{:S(2)}, u32[]{:S(2)}) %all-to-all-start.1) | async-done | bytes 3407904 | tf_op jit(solution)/shard_map/all_to_all | solution.py:83
  209.8 8.4 %reshape.277 = f32[4,16,8,52,32]{4,3,2,1,0:T(8,128)} reshape(f32[1,64,8,1664]{3,2,0,1:T(8,128)S(1)} %all-to-all-done.1) | data formatting | bytes 6815744 | tf_op jit(solution)/shard_map/reshape | solution.py:84
  218.2 14.6 %copy.36 = f32[4,16,8,52,32]{3,0,4,2,1:T(4,128)} copy(f32[4,16,8,52,32]{4,3,2,1,0:T(8,128)} %reshape.277) | data formatting | bytes 6815744 | tf_op jit(solution)/shard_map/reshape | solution.py:84
  232.8 22.1 %abs_reduce_fusion = (f32[16,8,52]{2,1,0:T(8,128)S(1)}, f32[16,8,52,4,32]{2,3,4,1,0:T(4,128)}) fusion(f32[4,16,8,52,32]{3,0,4,2,1:T(4,128)} %copy.36, s32[4]{0:T(128)S(1)} %get-tuple-element.22, s32[4]{0:T(128)S(1)} %get-tuple-element.23), kind=kOutput, calls=%fused_computation.2 | convolution fusion | flops 43443824 | bytes 6842400 | tf_op jit(solution)/shard_map/qg,gmnaj->mnaqj/dot_general | solution.py:85
  254.9 0.1 reduce_max.15
  255.0 0.1 reduce_max.20
  255.1 0.0 copy-start.1
  255.2 0.1 broadcast_bitcast_fusion
  255.2 11.5 %copy.37 = f32[16,8,52,4,32]{2,1,0,4,3:T(8,128)} copy(f32[16,8,52,4,32]{2,3,4,1,0:T(4,128)} %get-tuple-element.9) | data formatting | bytes 6815744 | tf_op jit(solution)/shard_map/mul | solution.py:87
  266.7 0.0 copy-done.1
  266.7 7.8 %mul.383 = f32[6656,128]{0,1:T(8,128)S(1)} reshape(f32[16,8,52,4,32]{2,1,0,4,3:T(8,128)} %copy.37) | data formatting | bytes 6815744 | tf_op jit(solution)/shard_map/mul | solution.py:87
  274.5 1.4 divide_convert_fusion
  275.9 3.8 %copy.38 = bf16[6656,128]{1,0:T(8,128)(2,1)} copy(bf16[6656,128]{0,1:T(8,128)(2,1)} %divide_convert_fusion) | data formatting | bytes 3407872
  (10 shorter events, 0.0 us)
Async XLA Ops:
  11.4 8.0 %copy-start = (f32[52,52,1,1]{1,0,3,2:T(8,128)S(1)}, f32[52,52,1,1]{1,0,3,2:T(8,128)}, u32[]{:S(2)}) copy-start(f32[52,52,1,1]{1,0,3,2:T(8,128)} %constant.2) | copy-start | bytes 32452
  164.3 45.5 %all-to-all-start.1 = ((f32[1,64,8,1664]{3,2,0,1:T(8,128)}), f32[1,64,8,1664]{3,2,0,1:T(8,128)S(1)}, u32[]{:S(2)}, u32[]{:S(2)}) async-start(f32[1,64,8,1664]{3,2,0,1:T(8,128)} %copy.35), calls=%async_computation.1 | async-start | bytes 6815744 | tf_op jit(solution)/shard_map/all_to_all | solution.py:83
  255.1 11.6 %copy-start.1 = (f32[52]{0:T(128)}, f32[52]{0:T(128)S(1)}, u32[]{:S(2)}) copy-start(f32[52]{0:T(128)S(1)} %reduce_max.20) | copy-start | bytes 628
where the time goes:
time: 285 us; the launch traced here: 280 us
  blocking collectives  93.5 us (33%)
  matrix products  71.2 us (25%)
  local copies, waits for them, and re-layouts  67.2 us (24%)
  waiting for transfers between devices  38.7 us (14%)
  starting transfers between devices  6.78 us (2%)
    all_to_all x1, blocking collectives, body(): lax.all_to_all(rotated, 'fsdp', split_axis=0, concat_axis=0, tiled=True)  93.5 us
    all_to_all x1, waiting for transfers between devices, body(): lax.all_to_all(stacked, 'grp', split_axis=1, concat_axis=0, tiled=True)  38.7 us
    dot_general x1, matrix products, body(): rotated = jnp.einsum('ab,pcbj->pcaj', paley, rotated, precision=exact_prec)  27 us
    reshape x2, local copies, waits for them, and re-layouts, body(): moved = moved.reshape(groups, parts // groups, count, 52, piece)  23 us
    dot_general x1, matrix products, body(): jnp.einsum('qg,gmnaj->mnaqj', group_signs, moved, precision=exact_prec)  22.1 us
    mul x2, local copies, waits for them, and re-layouts, body(): final = result.reshape(-1, cols_out) * (1.0 / math.sqrt(FF * D))  19.3 us
    dot_general x1, matrix products, body(): jnp.einsum('ce,peaj->pcaj', sub_signs, rotated, precision=exact_prec)  10.6 us
    reshape x1, local copies, waits for them, and re-layouts, body(): rotated = rotated.reshape(parts, sub_rows, 52, piece)  8.02 us
  transfers between devices with their start and end apart: 1, of which 1 were waited for; matrix products, arithmetic and copies ran while one was open for 0% of the time, Pallas kernels for 0%

commit v1 on v0

v1 whole, which is shorter than its diff:
```python
import functools
import math

import jax
import jax.numpy as jnp
import numpy as np
from jax import lax
from jax.experimental import pallas as pl
from jax.experimental.pallas import tpu as pltpu
from jax.sharding import PartitionSpec as P

MESH = pl.DeviceIdType.MESH
D = 8192
BLOCK = 128
FF = 26624
N_F = 64
N_G = 4
ROWS = FF // N_F
COLS = D // N_G
SUB = ROWS // 4
COEF = 1.0 / math.sqrt(FF * D)
CHUNKS = ((0, 32), (32, 32), (64, 24), (88, 16))


def paley_signs():
    squares_set = set()
    for coord_one in range(5):
        for coord_two in range(5):
            if coord_one or coord_two:
                squares_set.add(
                    (
                        (coord_one * coord_one + 2 * coord_two * coord_two) % 5,
                        2 * coord_one * coord_two % 5,
                    )
                )
    conference = np.zeros((26, 26), np.float32)
    conference[0, 1:] = 1.0
    conference[1:, 0] = 1.0
    for row_elem in range(25):
        for col_elem in range(25):
            diff_one = (row_elem % 5 - col_elem % 5) % 5
            diff_two = (row_elem // 5 - col_elem // 5) % 5
            if diff_one or diff_two:
                conference[1 + row_elem, 1 + col_elem] = (
                    1.0 if (diff_one, diff_two) in squares_set else -1.0
                )
    plus_block = np.array([[1.0, 1.0], [1.0, -1.0]], np.float32)
    minus_block = np.array([[1.0, -1.0], [-1.0, -1.0]], np.float32)
    return np.kron(conference, plus_block) + np.kron(np.eye(26), minus_block)


def sylvester(order):
    signs = np.ones((1, 1), np.float32)
    while signs.shape[0] < order:
        signs = np.kron(np.array([[1.0, 1.0], [1.0, -1.0]]), signs)
    return signs


def butterflies(values):
    values = list(values)
    step = 1
    while step < len(values):
        for i in range(len(values)):
            if not i & step:
                a, b = values[i], values[i | step]
                values[i], values[i | step] = a + b, a - b
        step *= 2
    return values


def block_transpose(h, low_half, even_block):
    out = list(h)
    for a in (0, 1):
        t = pltpu.roll(jnp.where(low_half, h[a + 2], h[a]), 64, 1)
        out[a] = jnp.where(low_half, h[a], t)
        out[a + 2] = jnp.where(low_half, t, h[a + 2])
    h, out = out, list(out)
    for a in (0, 2):
        out[a] = jnp.where(even_block, h[a], pltpu.roll(h[a + 1], 32, 1))
        out[a + 1] = jnp.where(even_block, pltpu.roll(h[a], 96, 1), h[a + 1])
    return out


def kernel(
    w_hbm, l_hbm, s_hbm, q_hbm, scale_ref,
    w, l, s256, x, s1, r1, z, g, o, m8, inv, qv,
    load_sem, send1, recv1, send2, recv2, out_sem,
):
    me_f, me_g = lax.axis_index("fsdp"), lax.axis_index("grp")
    loads = [
        pltpu.make_async_copy(src, dst, load_sem.at[i])
        for i, (src, dst) in enumerate(((w_hbm, w), (l_hbm, l), (s_hbm, s256)))
    ]
    for copy in loads:
        copy.start()

    def peer(i):
        k, rest = i % 8, i // 8
        odd = k % 2
        dz = odd * ((k + 1) // 2) + (1 - odd) * (8 - k // 2)
        dx, dy = rest // 4, rest % 4
        px = (me_f // 32 + dx) % 2
        pz = ((me_f // 4) % 8 + dz) % 8
        py = (me_f % 4 + dy) % 4
        return px * 32 + pz * 4 + py

    barrier = pltpu.get_barrier_semaphore()

    @pl.loop(1, N_F)
    def _(i):
        pl.semaphore_signal(barrier, inc=1, device_id=(peer(i), me_g), device_id_type=MESH)

    @pl.loop(1, N_G)
    def _(i):
        pl.semaphore_signal(barrier, inc=1, device_id=(me_f, (me_g + i) % N_G), device_id_type=MESH)

    lane = lax.broadcasted_iota(jnp.int32, (8, 128), 1)
    low_half = lane < 64
    even_block = (lane // 32) % 2 == 0
    m8[...] = jnp.zeros_like(m8)
    for copy in loads:
        copy.wait()

    def local_part(r0, n):
        lhs = l[4 * r0 : 4 * (r0 + n), :]
        for u in range(8):
            cols = slice(256 * u, 256 * (u + 1))
            part = jnp.dot(lhs, w[:, cols], preferred_element_type=jnp.float32)
            hi = part.astype(jnp.bfloat16)
            lo = (part - hi.astype(jnp.float32)).astype(jnp.bfloat16)
            x[u, : 4 * n, :] = jnp.dot(
                hi, s256[...], preferred_element_type=jnp.float32
            ) + jnp.dot(lo, s256[...], preferred_element_type=jnp.float32)

        @pl.loop(0, n // 8)
        def _(k):
            row = pl.multiple_of(k * 8, 8)
            for half in range(2):
                lanes = slice(128 * half, 128 * (half + 1))
                got = [
                    butterflies([x[u, pl.ds(row + a * n, 8), lanes] for u in range(8)])
                    for a in range(4)
                ]
                for u in range(8):
                    parts = block_transpose([got[a][u] for a in range(4)], low_half, even_block)
                    for b in range(4):
                        s1[(u * 2 + half) * 4 + b, pl.ds(r0 + row, 8), :] = parts[b]

    def send_fsdp(c, r0, n):
        rows = pl.ds(r0, n)
        pltpu.make_async_copy(s1.at[me_f, rows], r1.at[me_f, rows], recv1.at[c]).start()

        @pl.loop(1, N_F)
        def _(i):
            p = peer(i)
            pltpu.make_async_remote_copy(
                src_ref=s1.at[p, rows],
                dst_ref=r1.at[me_f, rows],
                send_sem=send1.at[c],
                recv_sem=recv1.at[c],
                device_id=(p, me_g),
                device_id_type=MESH,
            ).start()

    def fsdp_part(c, r0, n):
        rows = pl.ds(r0, n)
        pltpu.make_async_copy(r1.at[:, rows], r1.at[:, rows], recv1.at[c]).wait()

        @pl.loop(0, n // 8)
        def _(k):
            row = pl.ds(pl.multiple_of(r0 + k * 8, 8), 8)
            for a in range(8):
                got = butterflies([r1[a * 8 + b, row, :] for b in range(8)])
                for b in range(8):
                    z[a * 8 + b, row, :] = got[b]
            for b in range(8):
                got = butterflies([z[a * 8 + b, row, :] for a in range(8)])
                for a in range(8):
                    z[a * 8 + b, row, :] = got[a]

    def send_grp(c, r0, n):
        rows = pl.ds(r0, n)
        pltpu.make_async_copy(
            z.at[pl.ds(me_g * 16, 16), rows], g.at[me_g, :, rows], recv2.at[c]
        ).start()

        @pl.loop(1, N_G)
        def _(i):
            q = (me_g + i) % N_G
            pltpu.make_async_remote_copy(
                src_ref=z.at[pl.ds(q * 16, 16), rows],
                dst_ref=g.at[me_g, :, rows],
                send_sem=send2.at[c],
                recv_sem=recv2.at[c],
                device_id=(me_f, q),
                device_id_type=MESH,
            ).start()

    def grp_part(c, r0, n):
        rows = pl.ds(r0, n)
        pltpu.make_async_copy(g.at[:, :, rows], g.at[:, :, rows], recv2.at[c]).wait()

        @pl.loop(0, 16)
        def _(m):
            for k in range(n // 8):
                tile = r0 // 8 + k
                row = pl.ds(tile * 8, 8)
                got = butterflies([g[a, m, row, :] for a in range(4)])
                parts = block_transpose(got, low_half, even_block)
                for b in range(4):
                    at = (m * 4 + b) * (SUB // 8) + tile
                    o[pl.ds(pl.multiple_of(at * 8, 8), 8), :] = parts[b]
                    m8[at // 16] = jnp.maximum(m8[at // 16], jnp.abs(parts[b]))

    last = len(CHUNKS) - 1
    local_part(*CHUNKS[0])
    pl.semaphore_wait(barrier, N_F + N_G - 2)
    send_fsdp(0, *CHUNKS[0])
    for c in range(1, last + 1):
        local_part(*CHUNKS[c])
        send_fsdp(c, *CHUNKS[c])
    for c in range(last + 1):
        fsdp_part(c, *CHUNKS[c])
        send_grp(c, *CHUNKS[c])
        if c:
            grp_part(c - 1, *CHUNKS[c - 1])
    grp_part(last, *CHUNKS[last])

    top = jnp.max(jnp.max(m8[...], axis=1), axis=1, keepdims=True) * COEF
    scale_ref[...] = top
    inv[...] = jnp.broadcast_to(COEF / (top + 1e-06), (52, 128))
    quarter = 52 // 4
    outs = []
    for part in range(4):

        @pl.loop(part * quarter, (part + 1) * quarter)
        def _(i):
            rows = pl.ds(pl.multiple_of(i * BLOCK, BLOCK), BLOCK)
            qv[rows, :] = (o[rows, :] * inv[pl.ds(i, 1), :]).astype(jnp.bfloat16)

        rows = pl.ds(part * quarter * BLOCK, quarter * BLOCK)
        outs.append(pltpu.make_async_copy(qv.at[rows], q_hbm.at[rows], out_sem.at[part]))
        outs[-1].start()
    for copy in outs:
        copy.wait()
    for c, (r0, n) in enumerate(CHUNKS):
        sent = s1.at[pl.ds(0, N_F - 1), pl.ds(r0, n)]
        pltpu.make_async_copy(sent, sent, send1.at[c]).wait()
        sent = z.at[pl.ds(0, 48), pl.ds(r0, n)]
        pltpu.make_async_copy(sent, sent, send2.at[c]).wait()


def body(weight):
    full = np.kron(sylvester(8), paley_signs())
    order = np.concatenate(
        [a * SUB + np.arange(r0, r0 + n) for r0, n in CHUNKS for a in range(4)]
    )
    left = jnp.asarray(full[order], jnp.bfloat16)
    right = jnp.asarray(sylvester(256), jnp.bfloat16)
    count = len(CHUNKS)
    f32, bf16 = jnp.float32, jnp.bfloat16
    top_rows = 4 * max(n for _, n in CHUNKS)
    dma = pltpu.SemaphoreType.DMA
    return pl.pallas_call(
        kernel,
        out_shape=(
            jax.ShapeDtypeStruct((FF // N_G, D // N_F), bf16),
            jax.ShapeDtypeStruct((52, 1), f32),
        ),
        in_specs=[pl.BlockSpec(memory_space=pl.ANY)] * 3,
        out_specs=(
            pl.BlockSpec(memory_space=pl.ANY),
            pl.BlockSpec(memory_space=pltpu.VMEM),
        ),
        scratch_shapes=[
            pltpu.VMEM((ROWS, COLS), bf16),
            pltpu.VMEM((ROWS, ROWS), bf16),
            pltpu.VMEM((256, 256), bf16),
            pltpu.VMEM((8, top_rows, 256), f32),
            pltpu.VMEM((N_F, SUB, 128), f32),
            pltpu.VMEM((N_F, SUB, 128), f32),
            pltpu.VMEM((N_F, SUB, 128), f32),
            pltpu.VMEM((N_G, 16, SUB, 128), f32),
            pltpu.VMEM((FF // N_G, 128), f32),
            pltpu.VMEM((52, 8, 128), f32),
            pltpu.VMEM((52, 128), f32),
            pltpu.VMEM((FF // N_G, 128), bf16),
            dma((3,)),
            dma((count,)),
            dma((count,)),
            dma((count,)),
            dma((count,)),
            dma((4,)),
        ],
        compiler_params=pltpu.CompilerParams(
            collective_id=0, has_side_effects=True, vmem_limit_bytes=56 << 20
        ),
        name="rotate",
    )(weight, left, right)


def solution(mesh):
    in_specs = (P("fsdp", "grp"),)
    out_specs = (P("grp", "fsdp"), P("grp", "fsdp"))
    return jax.shard_map(body, mesh=mesh, in_specs=in_specs, out_specs=out_specs, check_vma=False)
```

time: 285 us -> 112 us (0.39); the launches traced: 280 us -> 111 us
  Pallas kernels: 0 us -> 107 us
  blocking collectives: 93.5 us -> 0 us
  matrix products: 71.2 us -> 0 us
  local copies, waits for them, and re-layouts: 67.2 us -> 4.08 us
  waiting for transfers between devices: 38.7 us -> 0 us
  starting transfers between devices: 6.78 us -> 0 us
    pallas_call x0 -> x1, Pallas kernels: none -> 107 us  [body(): pl.pallas_call(kernel, out_shape=(jax.ShapeDtypeStruct((FF // N_G, D // N...]
    all_to_all x1 -> x0, blocking collectives: 93.5 us -> none  [body(): lax.all_to_all(rotated, 'fsdp', split_axis=0, concat_axis=0, tiled=True)]
    dot_general x6 -> x0, matrix products: 71.2 us -> none  [the longest x1 27 us: body(): rotated = jnp.einsum('ab,pcbj->pcaj', paley, rotated, precision=exact_prec)]
    reshape x5 -> x0, local copies, waits for them, and re-layouts: 41.2 us -> none  [the longest x2 23 us: body(): moved = moved.reshape(groups, parts // groups, count, 52, piece)]
    all_to_all x1 -> x0, waiting for transfers between devices: 38.7 us -> none  [body(): lax.all_to_all(stacked, 'grp', split_axis=1, concat_axis=0, tiled=True)]
    mul x2 -> x0, local copies, waits for them, and re-layouts: 19.3 us -> none  [body(): final = result.reshape(-1, cols_out) * (1.0 / math.sqrt(FF * D))]
    all_to_all x1 -> x0, starting transfers between devices: 6.78 us -> none  [body(): lax.all_to_all(stacked, 'grp', split_axis=1, concat_axis=0, tiled=True)]
    unnamed x6 -> x1, local copies, waits for them, and re-layouts: 6.55 us -> 2.75 us
  transfers between devices with their start and end apart: 1 -> 0, of which waited for: 1 -> 0; matrix products, arithmetic and copies ran while one was open for 0% -> 0% of each run, Pallas kernels for 0% -> 0%
where the time goes in v1:
time: 112 us; the launch traced here: 111 us
  Pallas kernels  107 us (96%)
  local copies, waits for them, and re-layouts  4.08 us (4%)
    pallas_call x1, Pallas kernels, body(): pl.pallas_call(kernel, out_shape=(jax.ShapeDtypeStruct((FF // N_G, D // N...  107 us
    unnamed x1, local copies, waits for them, and re-layouts  2.75 us

profile of v1, /device:TPU:1, one launch (start us, length us, event | category | flops | bytes accessed | tf_op | source)
XLA Modules:
  0.0 111.3 jit_solution(9741572286521632738)
XLA Ops:
  0.6 106.6 %rotate.1 = (bf16[6656,128]{1,0:T(8,128)(2,1)}, f32[52,1]{1,0:T(8,128)}) custom-call(bf16[416,2048]{1,0:T(8,128)(2,1)} %w_hbm.1, bf16[416,416]{1,0:T(8,128)(2,1)} %constant.4.clone.l_hbm, bf16[256,256]{1,0:T(8,128)(2,1)} %constant.5.clone.s_hbm), custom_call_target="tpu_custom_call" | custom-call | tf_op jit(solution)/shard_map/rotate/pallas_call | solution.py:264
  107.3 1.3 %copy.5 = f32[52,1]{0,1:T(1,128)} copy(f32[52,1]{1,0:T(8,128)} %get-tuple-element.3) | data formatting | bytes 416 | tf_op jit(solution)/shard_map/rotate/pallas_call | solution.py:264
  108.6 2.7 %copy.7 = bf16[6656,128]{1,0:T(8,128)(2,1)} copy(bf16[6656,128]{1,0:T(8,128)(2,1)} %get-tuple-element.6) | data formatting | bytes 3407872

commit v2 on v1

v2 whole, which is shorter than its diff:
```python
import functools
import math

import jax
import jax.numpy as jnp
import numpy as np
from jax import lax
from jax.experimental import pallas as pl
from jax.experimental.pallas import tpu as pltpu
from jax.sharding import PartitionSpec as P

MESH = pl.DeviceIdType.MESH
D = 8192
BLOCK = 128
FF = 26624
N_F = 64
N_G = 4
ROWS = FF // N_F
COLS = D // N_G
SUB = ROWS // 4
COEF = 1.0 / math.sqrt(FF * D)
SIZES = (8, 8, 16, 16, 16, 16, 8, 8, 8)
FINISH = 26


def paley_signs():
    squares_set = set()
    for coord_one in range(5):
        for coord_two in range(5):
            if coord_one or coord_two:
                squares_set.add(
                    (
                        (coord_one * coord_one + 2 * coord_two * coord_two) % 5,
                        2 * coord_one * coord_two % 5,
                    )
                )
    conference = np.zeros((26, 26), np.float32)
    conference[0, 1:] = 1.0
    conference[1:, 0] = 1.0
    for row_elem in range(25):
        for col_elem in range(25):
            diff_one = (row_elem % 5 - col_elem % 5) % 5
            diff_two = (row_elem // 5 - col_elem // 5) % 5
            if diff_one or diff_two:
                conference[1 + row_elem, 1 + col_elem] = (
                    1.0 if (diff_one, diff_two) in squares_set else -1.0
                )
    plus_block = np.array([[1.0, 1.0], [1.0, -1.0]], np.float32)
    minus_block = np.array([[1.0, -1.0], [-1.0, -1.0]], np.float32)
    return np.kron(conference, plus_block) + np.kron(np.eye(26), minus_block)


def sylvester(order):
    signs = np.ones((1, 1), np.float32)
    while signs.shape[0] < order:
        signs = np.kron(np.array([[1.0, 1.0], [1.0, -1.0]]), signs)
    return signs


def chunks():
    starts = np.cumsum((0,) + tuple(SIZES))
    return [(int(a), n) for a, n in zip(starts, SIZES)]


def butterflies(values):
    values = list(values)
    step = 1
    while step < len(values):
        for i in range(len(values)):
            if not i & step:
                a, b = values[i], values[i | step]
                values[i], values[i | step] = a + b, a - b
        step *= 2
    return values


def block_transpose(h, low_half, even_block):
    out = list(h)
    for a in (0, 1):
        t = pltpu.roll(jnp.where(low_half, h[a + 2], h[a]), 64, 1)
        out[a] = jnp.where(low_half, h[a], t)
        out[a + 2] = jnp.where(low_half, t, h[a + 2])
    h, out = out, list(out)
    for a in (0, 2):
        out[a] = jnp.where(even_block, h[a], pltpu.roll(h[a + 1], 32, 1))
        out[a + 1] = jnp.where(even_block, pltpu.roll(h[a], 96, 1), h[a + 1])
    return out


def kernel(
    w_hbm, l_hbm, s_hbm, o, m8,
    w, l, s256, x, s1, r1, z, g,
    load_sem, send1, recv1, send2, recv2,
):
    me_f, me_g = lax.axis_index("fsdp"), lax.axis_index("grp")
    all_chunks = chunks()
    loads = [
        pltpu.make_async_copy(src, dst, load_sem.at[i])
        for i, (src, dst) in enumerate(((w_hbm, w), (l_hbm, l), (s_hbm, s256)))
    ]
    for copy in loads:
        copy.start()

    me_x, me_z, me_y = me_f // 32, me_f // 4 % 8, me_f % 4
    z_at = [((me_z + dz) % 8) * 4 for dz in (0, 1, 7, 2, 6, 3, 5, 4)]

    def each_peer(dx, step):
        base = (me_x + dx) % 2 * 32

        def row(dy, low):
            p_y = base + (me_y + dy) % 4
            for at in z_at[low:]:
                step(p_y + at)

        if dx == 0:
            row(0, 1)

        @pl.loop(1 - dx, 4)
        def _(dy):
            row(dy, 0)

    def piece(r0, n, first, count=1):
        return pl.ds(pl.multiple_of(N_F * r0 + first * n, 8), count * n)

    barrier = pltpu.get_barrier_semaphore()

    def greet(p):
        pl.semaphore_signal(barrier, inc=1, device_id=(p, me_g), device_id_type=MESH)

    each_peer(1, greet)
    each_peer(0, greet)

    @pl.loop(1, N_G)
    def _(i):
        pl.semaphore_signal(barrier, inc=1, device_id=(me_f, (me_g + i) % N_G), device_id_type=MESH)

    lane = lax.broadcasted_iota(jnp.int32, (8, 128), 1)
    low_half = lane < 64
    even_block = (lane // 32) % 2 == 0
    m8[...] = jnp.zeros_like(m8)
    for copy in loads:
        copy.wait()

    def local_part(r0, n):
        lhs = l[4 * r0 : 4 * (r0 + n), :]
        for u in range(8):
            cols = slice(256 * u, 256 * (u + 1))
            part = jnp.dot(lhs, w[:, cols], preferred_element_type=jnp.float32)
            hi = part.astype(jnp.bfloat16)
            lo = (part - hi.astype(jnp.float32)).astype(jnp.bfloat16)
            x[u, : 4 * n, :] = jnp.dot(
                hi, s256[...], preferred_element_type=jnp.float32
            ) + jnp.dot(lo, s256[...], preferred_element_type=jnp.float32)

        @pl.loop(0, n // 8)
        def _(k):
            row = pl.multiple_of(k * 8, 8)
            for half in range(2):
                lanes = slice(128 * half, 128 * (half + 1))
                got = [
                    butterflies([x[u, pl.ds(row + a * n, 8), lanes] for u in range(8)])
                    for a in range(4)
                ]
                for u in range(8):
                    parts = block_transpose([got[a][u] for a in range(4)], low_half, even_block)
                    for b in range(4):
                        at = N_F * r0 + ((u * 2 + half) * 4 + b) * n + row
                        s1[pl.ds(pl.multiple_of(at, 8), 8), :] = parts[b]

    def send_fsdp(c, dx):
        r0, n = all_chunks[c]
        mine = piece(r0, n, me_f)
        if dx == 0:
            pltpu.make_async_copy(s1.at[mine], r1.at[mine], recv1.at[c]).start()

        def send(p):
            pltpu.make_async_remote_copy(
                src_ref=s1.at[piece(r0, n, p)],
                dst_ref=r1.at[mine],
                send_sem=send1.at[c],
                recv_sem=recv1.at[c],
                device_id=(p, me_g),
                device_id_type=MESH,
            ).start()

        each_peer(dx, send)

    def fsdp_part(c, r0, n):
        whole = r1.at[piece(r0, n, 0, N_F)]
        pltpu.make_async_copy(whole, whole, recv1.at[c]).wait()

        @pl.loop(0, n // 8)
        def _(k):
            def tile(i):
                return pl.ds(pl.multiple_of(N_F * r0 + i * n + k * 8, 8), 8)

            for a in range(8):
                got = butterflies([r1[tile(a * 8 + b), :] for b in range(8)])
                for b in range(8):
                    z[tile(a * 8 + b), :] = got[b]
            for b in range(8):
                got = butterflies([z[tile(a * 8 + b), :] for a in range(8)])
                for a in range(8):
                    z[tile(a * 8 + b), :] = got[a]

    def send_grp(c, r0, n):
        mine = piece(r0, n, me_g * 16, 16)
        pltpu.make_async_copy(z.at[mine], g.at[mine], recv2.at[c]).start()

        @pl.loop(1, N_G)
        def _(i):
            q = (me_g + i) % N_G
            pltpu.make_async_remote_copy(
                src_ref=z.at[piece(r0, n, q * 16, 16)],
                dst_ref=g.at[mine],
                send_sem=send2.at[c],
                recv_sem=recv2.at[c],
                device_id=(me_f, q),
                device_id_type=MESH,
            ).start()

    def grp_part(c, r0, n):
        whole = g.at[piece(r0, n, 0, N_F)]
        pltpu.make_async_copy(whole, whole, recv2.at[c]).wait()

        @pl.loop(0, 16)
        def _(m):
            for k in range(n // 8):
                tile = r0 // 8 + k
                got = butterflies(
                    [
                        g[pl.ds(pl.multiple_of(N_F * r0 + (a * 16 + m) * n + k * 8, 8), 8), :]
                        for a in range(4)
                    ]
                )
                parts = block_transpose(got, low_half, even_block)
                for b in range(4):
                    at = (m * 4 + b) * (SUB // 8) + tile
                    o[pl.ds(pl.multiple_of(at * 8, 8), 8), :] = parts[b]
                    m8[at // 16] = jnp.maximum(m8[at // 16], jnp.abs(parts[b]))

    last = len(all_chunks) - 1
    for c in range(last + 1):
        local_part(*all_chunks[c])
        if c == 0:
            pl.semaphore_wait(barrier, N_F + N_G - 2)
        send_fsdp(c, 1)
        send_fsdp(c, 0)
    for c in range(last + 1):
        fsdp_part(c, *all_chunks[c])
        send_grp(c, *all_chunks[c])
        if c:
            grp_part(c - 1, *all_chunks[c - 1])
    grp_part(last, *all_chunks[last])

    for c, (r0, n) in enumerate(all_chunks):
        sent = s1.at[piece(r0, n, 0, N_F - 1)]
        pltpu.make_async_copy(sent, sent, send1.at[c]).wait()
        sent = z.at[piece(r0, n, 0, 48)]
        pltpu.make_async_copy(sent, sent, send2.at[c]).wait()


def finish(o, m8, q_ref, scale_ref):
    first = pl.program_id(0) * FINISH
    lane = lax.broadcasted_iota(jnp.int32, scale_ref.shape, 1)
    tops = scale_ref[...]
    for i in range(FINISH):
        block = first + i
        top = jnp.max(jnp.max(m8[block], axis=0, keepdims=True), axis=1, keepdims=True) * COEF
        tops = jnp.where(lane == block, top, tops)
        rows = pl.ds(pl.multiple_of(block * BLOCK, BLOCK), BLOCK)
        q_ref[BLOCK * i : BLOCK * (i + 1), :] = (o[rows, :] * (COEF / (top + 1e-06))).astype(
            jnp.bfloat16
        )
    scale_ref[...] = tops


def body(weight):
    full = np.kron(sylvester(8), paley_signs())
    order = np.concatenate(
        [a * SUB + np.arange(r0, r0 + n) for r0, n in chunks() for a in range(4)]
    )
    left = jnp.asarray(full[order], jnp.bfloat16)
    right = jnp.asarray(sylvester(256), jnp.bfloat16)
    count = len(SIZES)
    f32, bf16 = jnp.float32, jnp.bfloat16
    rows_out = FF // N_G
    blocks = rows_out // BLOCK
    dma = pltpu.SemaphoreType.DMA
    mixed, tops = pl.pallas_call(
        kernel,
        out_shape=(pltpu.VMEM((rows_out, 128), f32), pltpu.VMEM((blocks, 8, 128), f32)),
        in_specs=[pl.BlockSpec(memory_space=pltpu.HBM)] * 3,
        out_specs=(pl.BlockSpec(memory_space=pltpu.VMEM),) * 2,
        scratch_shapes=[
            pltpu.VMEM((ROWS, COLS), bf16),
            pltpu.VMEM((ROWS, ROWS), bf16),
            pltpu.VMEM((256, 256), bf16),
            pltpu.VMEM((8, 4 * max(SIZES), 256), f32),
            *[pltpu.VMEM((N_F * SUB, 128), f32)] * 4,
            dma((3,)),
            *[dma((count,))] * 4,
        ],
        compiler_params=pltpu.CompilerParams(
            collective_id=0, has_side_effects=True, vmem_limit_bytes=60 << 20
        ),
        name="rotate",
    )(weight, left, right)
    quantized, scales = pl.pallas_call(
        finish,
        grid=(blocks // FINISH,),
        out_shape=(
            jax.ShapeDtypeStruct((rows_out, 128), bf16),
            jax.ShapeDtypeStruct((1, blocks), f32),
        ),
        in_specs=[pl.BlockSpec(memory_space=pltpu.VMEM)] * 2,
        out_specs=(
            pl.BlockSpec((FINISH * BLOCK, 128), lambda i: (i, 0)),
            pl.BlockSpec((1, blocks), lambda i: (0, 0)),
        ),
        compiler_params=pltpu.CompilerParams(vmem_limit_bytes=16 << 20),
        name="finish",
    )(mixed, tops)
    return quantized, scales.reshape(blocks, 1)


def solution(mesh):
    in_specs = (P("fsdp", "grp"),)
    out_specs = (P("grp", "fsdp"), P("grp", "fsdp"))
    return jax.shard_map(body, mesh=mesh, in_specs=in_specs, out_specs=out_specs, check_vma=False)
```

time: 112 us -> 99.3 us (0.89)
  Pallas kernels: 107 us -> 98.5 us
  local copies, waits for them, and re-layouts: 4.08 us -> 0 us
    pallas_call x1 -> x2, Pallas kernels: 107 us -> 98.5 us  [the longest x1 97.1 us: body(): pl.pallas_call(kernel, out_shape=(pltpu.VMEM((rows_out, 128), f32), pltpu...]
    unnamed x1 -> x0, local copies, waits for them, and re-layouts: 2.75 us -> none
    pallas_call x1 -> x0, local copies, waits for them, and re-layouts: 1.33 us -> none  [body(): pl.pallas_call(kernel, out_shape=(jax.ShapeDtypeStruct((FF // N_G, D // N...]
where the time goes in v2:
time: 99.3 us; the launch traced here: 99.1 us
  Pallas kernels  98.5 us (99%)
    pallas_call x1, Pallas kernels, body(): pl.pallas_call(kernel, out_shape=(pltpu.VMEM((rows_out, 128), f32), pltpu...  97.1 us

profile of v2, /device:TPU:1, one launch (start us, length us, event | category | flops | bytes accessed | tf_op | source)
XLA Modules:
  0.0 99.1 jit_solution(17877750838626893310)
XLA Ops:
  0.6 97.1 %rotate.1 = (f32[6656,128]{1,0:T(8,128)S(1)}, f32[52,8,128]{2,1,0:T(8,128)S(1)}) custom-call(bf16[416,2048]{1,0:T(8,128)(2,1)} %w_hbm.1, bf16[416,416]{1,0:T(8,128)(2,1)} %constant.4.clone.l_hbm, bf16[256,256]{1,0:T(8,128)(2,1)} %constant.5.clone.s_hbm), custom_call_target="tpu_custom_call" | custom-call | tf_op jit(solution)/shard_map/rotate/pallas_call | solution.py:290
  97.7 1.4 %finish.1 = (bf16[6656,128]{1,0:T(8,128)(2,1)}, f32[1,52]{1,0:T(1,128)}) custom-call(f32[6656,128]{1,0:T(8,128)S(1)} %get-tuple-element.6.o, f32[52,8,128]{2,1,0:T(8,128)S(1)} %get-tuple-element.7.m8), custom_call_target="tpu_custom_call" | custom-call | tf_op jit(solution)/shard_map/finish/pallas_call | solution.py:309

commit v3 on v2

--- a/solution.py
+++ b/solution.py
@@ -1,4 +1,4 @@
-import functools
+import itertools
 import math
 
 import jax
@@ -21,6 +21,10 @@
 COEF = 1.0 / math.sqrt(FF * D)
 SIZES = (8, 8, 16, 16, 16, 16, 8, 8, 8)
 FINISH = 26
+Z_ORDER = (1, 7, 2, 6, 3, 5, 4, 0)
+LEAD = 4
+LAG = 1
+GROUP = 4
 
 
 def paley_signs():
@@ -88,7 +92,7 @@
 
 
 def kernel(
-    w_hbm, l_hbm, s_hbm, o, m8,
+    w_hbm, l_hbm, s_hbm, o,
     w, l, s256, x, s1, r1, z, g,
     load_sem, send1, recv1, send2, recv2,
 ):
@@ -102,22 +106,21 @@
         copy.start()
 
     me_x, me_z, me_y = me_f // 32, me_f // 4 % 8, me_f % 4
-    z_at = [((me_z + dz) % 8) * 4 for dz in (0, 1, 7, 2, 6, 3, 5, 4)]
+    z_at = [((me_z + dz) % 8) * 4 for dz in Z_ORDER]
 
     def each_peer(dx, step):
         base = (me_x + dx) % 2 * 32
 
-        def row(dy, low):
+        def row(dy, ats):
             p_y = base + (me_y + dy) % 4
-            for at in z_at[low:]:
+            for at in ats:
                 step(p_y + at)
 
-        if dx == 0:
-            row(0, 1)
-
-        @pl.loop(1 - dx, 4)
-        def _(dy):
-            row(dy, 0)
+        @pl.loop(0, 3)
+        def _(i):
+            row(2 + i + i // 2, z_at)
+
+        row(0, z_at if dx else z_at[:-1])
 
     def piece(r0, n, first, count=1):
         return pl.ds(pl.multiple_of(N_F * r0 + first * n, 8), count * n)
@@ -137,7 +140,6 @@
     lane = lax.broadcasted_iota(jnp.int32, (8, 128), 1)
     low_half = lane < 64
     even_block = (lane // 32) % 2 == 0
-    m8[...] = jnp.zeros_like(m8)
     for copy in loads:
         copy.wait()
 
@@ -207,9 +209,7 @@
         mine = piece(r0, n, me_g * 16, 16)
         pltpu.make_async_copy(z.at[mine], g.at[mine], recv2.at[c]).start()
 
-        @pl.loop(1, N_G)
-        def _(i):
-            q = (me_g + i) % N_G
+        def send(q):
             pltpu.make_async_remote_copy(
                 src_ref=z.at[piece(r0, n, q * 16, 16)],
                 dst_ref=g.at[mine],
@@ -219,40 +219,45 @@
                 device_id_type=MESH,
             ).start()
 
+        core, chip = me_g % 2, me_g // 2
+        send((1 - chip) * 2 + core)
+        send((1 - chip) * 2 + 1 - core)
+        send(chip * 2 + 1 - core)
+
     def grp_part(c, r0, n):
         whole = g.at[piece(r0, n, 0, N_F)]
         pltpu.make_async_copy(whole, whole, recv2.at[c]).wait()
 
-        @pl.loop(0, 16)
-        def _(m):
-            for k in range(n // 8):
-                tile = r0 // 8 + k
+        @pl.loop(0, 16 // GROUP)
+        def _(step):
+            done = []
+            for m, k in itertools.product(range(GROUP), range(n // 8)):
+                m = step * GROUP + m
                 got = butterflies(
                     [
                         g[pl.ds(pl.multiple_of(N_F * r0 + (a * 16 + m) * n + k * 8, 8), 8), :]
                         for a in range(4)
                     ]
                 )
-                parts = block_transpose(got, low_half, even_block)
+                at = m * 4 * SUB + r0 + k * 8
+                done.append((at, block_transpose(got, low_half, even_block)))
+            for at, parts in done:
                 for b in range(4):
-                    at = (m * 4 + b) * (SUB // 8) + tile
-                    o[pl.ds(pl.multiple_of(at * 8, 8), 8), :] = parts[b]
-                    m8[at // 16] = jnp.maximum(m8[at // 16], jnp.abs(parts[b]))
-
-    last = len(all_chunks) - 1
-    for c in range(last + 1):
-        local_part(*all_chunks[c])
-        if c == 0:
-            pl.semaphore_wait(barrier, N_F + N_G - 2)
-        send_fsdp(c, 1)
-        send_fsdp(c, 0)
-    for c in range(last + 1):
-        fsdp_part(c, *all_chunks[c])
-        send_grp(c, *all_chunks[c])
-        if c:
-            grp_part(c - 1, *all_chunks[c - 1])
-    grp_part(last, *all_chunks[last])
-
+                    o[pl.ds(pl.multiple_of(at + b * SUB, 8), 8), :] = parts[b]
+
+    count = len(all_chunks)
+    for step in range(-LEAD, count + LAG):
+        if 0 <= step < count:
+            fsdp_part(step, *all_chunks[step])
+            send_grp(step, *all_chunks[step])
+        if step + LEAD < count:
+            local_part(*all_chunks[step + LEAD])
+            if step == -LEAD:
+                pl.semaphore_wait(barrier, N_F + N_G - 2)
+            send_fsdp(step + LEAD, 1)
+            send_fsdp(step + LEAD, 0)
+        if step >= LAG:
+            grp_part(step - LAG, *all_chunks[step - LAG])
     for c, (r0, n) in enumerate(all_chunks):
         sent = s1.at[piece(r0, n, 0, N_F - 1)]
         pltpu.make_async_copy(sent, sent, send1.at[c]).wait()
@@ -260,16 +265,17 @@
         pltpu.make_async_copy(sent, sent, send2.at[c]).wait()
 
 
-def finish(o, m8, q_ref, scale_ref):
+def finish(o, q_ref, scale_ref):
     first = pl.program_id(0) * FINISH
     lane = lax.broadcasted_iota(jnp.int32, scale_ref.shape, 1)
     tops = scale_ref[...]
     for i in range(FINISH):
         block = first + i
-        top = jnp.max(jnp.max(m8[block], axis=0, keepdims=True), axis=1, keepdims=True) * COEF
+        values = o[pl.ds(pl.multiple_of(block * BLOCK, BLOCK), BLOCK), :]
+        top = jnp.max(jnp.max(jnp.abs(values), axis=0, keepdims=True), axis=1, keepdims=True)
+        top = top * COEF
         tops = jnp.where(lane == block, top, tops)
-        rows = pl.ds(pl.multiple_of(block * BLOCK, BLOCK), BLOCK)
-        q_ref[BLOCK * i : BLOCK * (i + 1), :] = (o[rows, :] * (COEF / (top + 1e-06))).astype(
+        q_ref[BLOCK * i : BLOCK * (i + 1), :] = (values * (COEF / (top + 1e-06))).astype(
             jnp.bfloat16
         )
     scale_ref[...] = tops
@@ -287,11 +293,11 @@
     rows_out = FF // N_G
     blocks = rows_out // BLOCK
     dma = pltpu.SemaphoreType.DMA
-    mixed, tops = pl.pallas_call(
+    mixed = pl.pallas_call(
         kernel,
-        out_shape=(pltpu.VMEM((rows_out, 128), f32), pltpu.VMEM((blocks, 8, 128), f32)),
+        out_shape=pltpu.VMEM((rows_out, 128), f32),
         in_specs=[pl.BlockSpec(memory_space=pltpu.HBM)] * 3,
-        out_specs=(pl.BlockSpec(memory_space=pltpu.VMEM),) * 2,
+        out_specs=pl.BlockSpec(memory_space=pltpu.VMEM),
         scratch_shapes=[
             pltpu.VMEM((ROWS, COLS), bf16),
             pltpu.VMEM((ROWS, ROWS), bf16),
@@ -313,14 +319,14 @@
             jax.ShapeDtypeStruct((rows_out, 128), bf16),
             jax.ShapeDtypeStruct((1, blocks), f32),
         ),
-        in_specs=[pl.BlockSpec(memory_space=pltpu.VMEM)] * 2,
+        in_specs=[pl.BlockSpec(memory_space=pltpu.VMEM)],
         out_specs=(
             pl.BlockSpec((FINISH * BLOCK, 128), lambda i: (i, 0)),
             pl.BlockSpec((1, blocks), lambda i: (0, 0)),
         ),
         compiler_params=pltpu.CompilerParams(vmem_limit_bytes=16 << 20),
         name="finish",
-    )(mixed, tops)
+    )(mixed)
     return quantized, scales.reshape(blocks, 1)
 
 

time: 99.3 us -> 95.7 us (0.964)
  Pallas kernels: 98.5 us -> 94.9 us
    pallas_call x1, Pallas kernels: 97.1 us -> 93.5 us  [body(): pl.pallas_call(kernel, out_shape=pltpu.VMEM((rows_out, 128), f32), in_spe...]
where the time goes in v3:
time: 95.7 us; the launch traced here: 95.6 us
  Pallas kernels  94.9 us (99%)
    pallas_call x1, Pallas kernels, body(): pl.pallas_call(kernel, out_shape=pltpu.VMEM((rows_out, 128), f32), in_spe...  93.5 us

profile of v3, /device:TPU:1, one launch (start us, length us, event | category | flops | bytes accessed | tf_op | source)
XLA Modules:
  0.0 95.6 jit_solution(16304629134631024134)
XLA Ops:
  0.6 93.5 %rotate.1.o = f32[6656,128]{1,0:T(8,128)S(1)} custom-call(bf16[416,2048]{1,0:T(8,128)(2,1)} %w_hbm.1, bf16[416,416]{1,0:T(8,128)(2,1)} %constant.4.clone.l_hbm, bf16[256,256]{1,0:T(8,128)(2,1)} %constant.5.clone.s_hbm), custom_call_target="tpu_custom_call" | custom-call | tf_op jit(solution)/shard_map/rotate/pallas_call | solution.py:296
  94.1 1.4 %finish.1 = (bf16[6656,128]{1,0:T(8,128)(2,1)}, f32[1,52]{1,0:T(1,128)}) custom-call(f32[6656,128]{1,0:T(8,128)S(1)} %rotate.1.o), custom_call_target="tpu_custom_call" | custom-call | tf_op jit(solution)/shard_map/finish/pallas_call | solution.py:315

commit v4 on v3

--- a/solution.py
+++ b/solution.py
@@ -108,7 +108,7 @@
     me_x, me_z, me_y = me_f // 32, me_f // 4 % 8, me_f % 4
     z_at = [((me_z + dz) % 8) * 4 for dz in Z_ORDER]
 
-    def each_peer(dx, step):
+    def each_peer(dx, step, ats):
         base = (me_x + dx) % 2 * 32
 
         def row(dy, ats):
@@ -118,9 +118,9 @@
 
         @pl.loop(0, 3)
         def _(i):
-            row(2 + i + i // 2, z_at)
-
-        row(0, z_at if dx else z_at[:-1])
+            row(2 + i + i // 2, [*ats, z_at[-1]])
+
+        row(0, [*ats, z_at[-1]] if dx else ats)
 
     def piece(r0, n, first, count=1):
         return pl.ds(pl.multiple_of(N_F * r0 + first * n, 8), count * n)
@@ -130,8 +130,8 @@
     def greet(p):
         pl.semaphore_signal(barrier, inc=1, device_id=(p, me_g), device_id_type=MESH)
 
-    each_peer(1, greet)
-    each_peer(0, greet)
+    each_peer(1, greet, z_at[-2::-1])
+    each_peer(0, greet, z_at[-2::-1])
 
     @pl.loop(1, N_G)
     def _(i):
@@ -185,31 +185,34 @@
                 device_id_type=MESH,
             ).start()
 
-        each_peer(dx, send)
+        each_peer(dx, send, z_at[:-1])
 
     def fsdp_part(c, r0, n):
         whole = r1.at[piece(r0, n, 0, N_F)]
         pltpu.make_async_copy(whole, whole, recv1.at[c]).wait()
 
+        def tile(i, k):
+            return pl.ds(pl.multiple_of(N_F * r0 + i * n + k * 8, 8), 8)
+
         @pl.loop(0, n // 8)
         def _(k):
-            def tile(i):
-                return pl.ds(pl.multiple_of(N_F * r0 + i * n + k * 8, 8), 8)
-
-            for a in range(8):
-                got = butterflies([r1[tile(a * 8 + b), :] for b in range(8)])
-                for b in range(8):
-                    z[tile(a * 8 + b), :] = got[b]
             for b in range(8):
-                got = butterflies([z[tile(a * 8 + b), :] for a in range(8)])
+                got = butterflies([r1[tile(a * 8 + b, k), :] for a in range(8)])
                 for a in range(8):
-                    z[tile(a * 8 + b), :] = got[a]
-
-    def send_grp(c, r0, n):
+                    z[tile(a * 8 + b, k), :] = got[a]
+
         mine = piece(r0, n, me_g * 16, 16)
-        pltpu.make_async_copy(z.at[mine], g.at[mine], recv2.at[c]).start()
+
+        def block(q):
+            for k in range(n // 8):
+                for a in range(2):
+                    at = [tile(q * 16 + a * 8 + b, k) for b in range(8)]
+                    got = butterflies([z[i, :] for i in at])
+                    for i, value in zip(at, got):
+                        z[i, :] = value
 
         def send(q):
+            block(q)
             pltpu.make_async_remote_copy(
                 src_ref=z.at[piece(r0, n, q * 16, 16)],
                 dst_ref=g.at[mine],
@@ -223,6 +226,8 @@
         send((1 - chip) * 2 + core)
         send((1 - chip) * 2 + 1 - core)
         send(chip * 2 + 1 - core)
+        block(me_g)
+        pltpu.make_async_copy(z.at[mine], g.at[mine], recv2.at[c]).start()
 
     def grp_part(c, r0, n):
         whole = g.at[piece(r0, n, 0, N_F)]
@@ -249,7 +254,6 @@
     for step in range(-LEAD, count + LAG):
         if 0 <= step < count:
             fsdp_part(step, *all_chunks[step])
-            send_grp(step, *all_chunks[step])
         if step + LEAD < count:
             local_part(*all_chunks[step + LEAD])
             if step == -LEAD:

time: 95.7 us -> 95.5 us (level)
  no operation moved by 1% of the time
where the time goes in v4:
time: 95.5 us; the launch traced here: 95.4 us
  Pallas kernels  94.7 us (99%)
    pallas_call x1, Pallas kernels, body(): pl.pallas_call(kernel, out_shape=pltpu.VMEM((rows_out, 128), f32), in_spe...  93.3 us

profile of v4, /device:TPU:1, one launch (start us, length us, event | category | flops | bytes accessed | tf_op | source)
XLA Modules:
  0.0 95.4 jit_solution(16381832766145283412)
XLA Ops:
  0.6 93.3 %rotate.1.o = f32[6656,128]{1,0:T(8,128)S(1)} custom-call(bf16[416,2048]{1,0:T(8,128)(2,1)} %w_hbm.1, bf16[416,416]{1,0:T(8,128)(2,1)} %constant.4.clone.l_hbm, bf16[256,256]{1,0:T(8,128)(2,1)} %constant.5.clone.s_hbm), custom_call_target="tpu_custom_call" | custom-call | tf_op jit(solution)/shard_map/rotate/pallas_call | solution.py:300
  94.0 1.4 %finish.1 = (bf16[6656,128]{1,0:T(8,128)(2,1)}, f32[1,52]{1,0:T(1,128)}) custom-call(f32[6656,128]{1,0:T(8,128)S(1)} %rotate.1.o), custom_call_target="tpu_custom_call" | custom-call | tf_op jit(solution)/shard_map/finish/pallas_call | solution.py:319

commit v5 on v3

--- a/solution.py
+++ b/solution.py
@@ -20,7 +20,7 @@
 SUB = ROWS // 4
 COEF = 1.0 / math.sqrt(FF * D)
 SIZES = (8, 8, 16, 16, 16, 16, 8, 8, 8)
-FINISH = 26
+FINISH = 13
 Z_ORDER = (1, 7, 2, 6, 3, 5, 4, 0)
 LEAD = 4
 LAG = 1
@@ -265,20 +265,25 @@
         pltpu.make_async_copy(sent, sent, send2.at[c]).wait()
 
 
-def finish(o, q_ref, scale_ref):
-    first = pl.program_id(0) * FINISH
+def finish(o, q_hbm, scale_ref, qv, sems):
     lane = lax.broadcasted_iota(jnp.int32, scale_ref.shape, 1)
-    tops = scale_ref[...]
-    for i in range(FINISH):
-        block = first + i
-        values = o[pl.ds(pl.multiple_of(block * BLOCK, BLOCK), BLOCK), :]
+    tops = jnp.zeros(scale_ref.shape, jnp.float32)
+    copies = []
+    for block in range(scale_ref.shape[1]):
+        rows = slice(BLOCK * block, BLOCK * (block + 1))
+        values = o[rows, :]
         top = jnp.max(jnp.max(jnp.abs(values), axis=0, keepdims=True), axis=1, keepdims=True)
         top = top * COEF
         tops = jnp.where(lane == block, top, tops)
-        q_ref[BLOCK * i : BLOCK * (i + 1), :] = (values * (COEF / (top + 1e-06))).astype(
-            jnp.bfloat16
-        )
+        qv[rows, :] = (values * (COEF / (top + 1e-06))).astype(jnp.bfloat16)
+        if (block + 1) % FINISH == 0:
+            part = block // FINISH
+            done = pl.ds(part * FINISH * BLOCK, FINISH * BLOCK)
+            copies.append(pltpu.make_async_copy(qv.at[done], q_hbm.at[done], sems.at[part]))
+            copies[-1].start()
     scale_ref[...] = tops
+    for copy in copies:
+        copy.wait()
 
 
 def body(weight):
@@ -314,16 +319,19 @@
     )(weight, left, right)
     quantized, scales = pl.pallas_call(
         finish,
-        grid=(blocks // FINISH,),
         out_shape=(
             jax.ShapeDtypeStruct((rows_out, 128), bf16),
             jax.ShapeDtypeStruct((1, blocks), f32),
         ),
         in_specs=[pl.BlockSpec(memory_space=pltpu.VMEM)],
         out_specs=(
-            pl.BlockSpec((FINISH * BLOCK, 128), lambda i: (i, 0)),
-            pl.BlockSpec((1, blocks), lambda i: (0, 0)),
+            pl.BlockSpec(memory_space=pltpu.HBM),
+            pl.BlockSpec(memory_space=pltpu.VMEM),
         ),
+        scratch_shapes=[
+            pltpu.VMEM((rows_out, 128), bf16),
+            pltpu.SemaphoreType.DMA((blocks // FINISH,)),
+        ],
         compiler_params=pltpu.CompilerParams(vmem_limit_bytes=16 << 20),
         name="finish",
     )(mixed)

time: 95.7 us -> 96.2 us (level)
  no operation moved by 1% of the time
where the time goes in v5:
time: 96.2 us; the launch traced here: 96 us
  Pallas kernels  95.4 us (99%)
    pallas_call x1, Pallas kernels, body(): pl.pallas_call(kernel, out_shape=pltpu.VMEM((rows_out, 128), f32), in_spe...  93.5 us

profile of v5, /device:TPU:1, one launch (start us, length us, event | category | flops | bytes accessed | tf_op | source)
XLA Modules:
  0.0 96.0 jit_solution(2807741926939082979)
XLA Ops:
  0.6 93.5 %rotate.1.o = f32[6656,128]{1,0:T(8,128)S(1)} custom-call(bf16[416,2048]{1,0:T(8,128)(2,1)} %w_hbm.1, bf16[416,416]{1,0:T(8,128)(2,1)} %constant.4.clone.l_hbm, bf16[256,256]{1,0:T(8,128)(2,1)} %constant.5.clone.s_hbm), custom_call_target="tpu_custom_call" | custom-call | tf_op jit(solution)/shard_map/rotate/pallas_call | solution.py:301
  94.1 1.9 %finish.1 = (bf16[6656,128]{1,0:T(8,128)(2,1)}, f32[1,52]{1,0:T(1,128)}) custom-call(f32[6656,128]{1,0:T(8,128)S(1)} %rotate.1.o), custom_call_target="tpu_custom_call" | custom-call | tf_op jit(solution)/shard_map/finish/pallas_call | solution.py:320
